TPU v7x, 256 devices: a whole 4x4x8 slice. The times are simulated.
256 devices in a mesh: branch: 32 (over z, y_lo, core), bus: 8 (over x, y_hi).
Axes of the slice: x: 4, y: 4 (y_hi: 2, y_lo: 2; y = y_hi * 2 + y_lo), z: 8, core: 2. Of those that a mesh axis runs over, the one named last changes fastest.
Arguments:
- injections: float32 [512, 60416], P('branch', 'bus'), may hold values from -0.0234375 to 0.0234375
- ptdf_mon: float32 [4096, 60416], P('branch', 'bus'), may hold values from -2.5 to 2.5
- ptdf_out: float32 [2048, 60416], P('branch', 'bus'), may hold values from -2.5 to 2.5
- outage_from: int32 [2048], replicated, may hold values from 0 to 60415
- outage_to: int32 [2048], replicated, may hold values from 0 to 60415
- hour_ids: int32 [512], P('bus'), may hold values from 0 to 8759
- ratings: float32 [4096, 4], P('branch'), may hold values from 0.5 to 2
Outputs:
- worst_loading: float32 [512, 4096], P('bus', 'branch')
All inputs are finite; a program needn't handle non-finite values.
Results may differ from a plain program's by a relative error of at most 0.00019.
Values sent between devices are 32-bit elements; how exact they have to be, the bound alone decides.
A program may use at most 128 MiB of HBM per device.

v0:
```python
import jax
import jax.numpy as jnp
from jax import lax
from jax.sharding import PartitionSpec as P


def screen(base_mon, outage_base, lodf_t, block_size):
    outage_count = lodf_t.shape[0]

    def advance(index, worst_load):
        first = index * block_size
        lodf_block = lax.dynamic_slice_in_dim(lodf_t, first, block_size, 0)
        flow_block = lax.dynamic_slice_in_dim(outage_base, first, block_size, 1)
        after_outage = base_mon[:, None, :] + flow_block[:, :, None] * lodf_block[None, :, :]
        return jnp.maximum(worst_load, jnp.max(jnp.abs(after_outage), axis=1))

    return lax.fori_loop(0, outage_count // block_size, advance, jnp.abs(base_mon))


def on_device(injections, ptdf_mon, ptdf_out, outage_from, outage_to, hour_ids, ratings):
    highest = lax.Precision.HIGHEST
    mon_rows = ptdf_mon.shape[0]
    out_rows = ptdf_out.shape[0]
    bus_width = ptdf_mon.shape[1]
    bus_count = lax.axis_size("bus")
    bus_index = lax.axis_index("bus")
    contract = (((1,), (1,)), ((), ()))
    piece = lax.all_gather(injections, "branch", axis=0, tiled=True)
    monitored = lax.dot_general(
        piece, ptdf_mon, contract, precision=highest, preferred_element_type=jnp.float32
    )
    outaged = lax.dot_general(
        piece, ptdf_out, contract, precision=highest, preferred_element_type=jnp.float32
    )
    partial_flows = jnp.concatenate([monitored, outaged], axis=1)
    hours_dev = partial_flows.shape[0] // bus_count
    summed_flows = lax.psum(partial_flows, "bus")
    base_flows = lax.dynamic_slice_in_dim(summed_flows, bus_index * hours_dev, hours_dev, 0)
    offset = bus_index * bus_width

    def localize(bus_ids):
        shifted = bus_ids - offset
        inside = jnp.logical_and(shifted >= 0, shifted < bus_width).astype(jnp.float32)
        return (jnp.clip(shifted, 0, bus_width - 1), inside)

    from_index, from_inside = localize(outage_from)
    to_index, to_inside = localize(outage_to)

    def columns(matrix):
        return (
            jnp.take(matrix, from_index, axis=1) * from_inside[None, :]
            - jnp.take(matrix, to_index, axis=1) * to_inside[None, :]
        )

    first_outage = lax.axis_index("branch") * out_rows
    sens_mon, sens_out = lax.psum((columns(ptdf_mon), columns(ptdf_out)), "bus")
    self_sens = jnp.diagonal(lax.dynamic_slice_in_dim(sens_out, first_outage, out_rows, 1))
    base_mon = base_flows[:, :mon_rows]
    base_out = base_flows[:, mon_rows:]
    outage_base, outage_self = (
        lax.all_gather(base_out, "branch", axis=1, tiled=True),
        lax.all_gather(self_sens, "branch", axis=0, tiled=True),
    )
    divisor = jnp.maximum(1.0 - outage_self, 0.25)
    lodf_t = (sens_mon / divisor[None, :]).T
    worst_load = screen(base_mon, outage_base, lodf_t, min(256, lodf_t.shape[0]))
    season = hour_ids * 4 // 8760
    onehot = (season[:, None] == jnp.arange(ratings.shape[1], dtype=jnp.int32)[None, :]).astype(
        jnp.float32
    )
    hour_rating = jnp.dot(onehot, ratings.T, precision=highest, preferred_element_type=jnp.float32)
    return worst_load / hour_rating


def solution(mesh):
    placed = (
        P("branch", "bus"),
        P("branch", "bus"),
        P("branch", "bus"),
        P(),
        P(),
        P("bus"),
        P("branch", None),
    )
    return jax.shard_map(
        on_device, mesh=mesh, in_specs=placed, out_specs=P("bus", "branch"), check_vma=False
    )
```

profile of v0, /device:TPU:1, one launch (start us, length us, event | category | flops | bytes accessed | tf_op | source)
XLA Modules:
  0.0 395.7 jit_solution(17618373268766414951)
XLA Ops:
  6.5 0.0 copy-start
  6.5 0.0 all-gather.2.cloned.1.call-start
  6.5 0.7 all-gather.2.cloned.1.call-update
  7.3 0.0 all-reduce.4.cloned.1.call-start
  7.3 0.0 copy-start.7
  7.3 0.0 copy-start.8
  7.3 5.4 %copy.22 = f32[128,7552]{0,1:T(8,128)} copy(f32[128,7552]{1,0:T(8,128)} %param.14) | data formatting | bytes 7733248 | tf_op args[1]
  12.7 0.0 copy-done.7
  12.7 0.0 copy-done.8
  12.7 7.6 %gather_fusion.2 = f32[2048,128]{1,0:T(8,128)S(1)} fusion(f32[128,7552]{0,1:T(8,128)} %copy.22, s32[2048]{0:T(1024)S(1)} %get-tuple-element.139), kind=kCustom, calls=%fused_computation.2.clone | custom fusion | bytes 2105344 | tf_op jit(solution)/shard_map/jit(_take)/gather | solution.py:52
  20.3 0.0 copy-start.3
  20.3 9.8 %gather_fusion.1 = f32[2048,128]{1,0:T(8,128)} fusion(f32[128,7552]{0,1:T(8,128)} %copy.22, s32[2048]{0:T(1024)S(1)} %get-tuple-element.138), kind=kCustom, calls=%fused_computation.clone | custom fusion | bytes 2105344 | tf_op jit(solution)/shard_map/jit(_take)/gather | solution.py:51
  30.1 0.0 copy-done.3
  30.1 2.7 copy.24
  32.9 9.8 %gather_fusion.4 = f32[2048,64]{1,0:T(8,128)} fusion(f32[64,7552]{0,1:T(8,128)} %copy.24, s32[2048]{0:T(1024)S(1)} %get-tuple-element.139), kind=kCustom, calls=%fused_computation.3.clone | custom fusion | bytes 1056768 | tf_op jit(solution)/shard_map/jit(_take)/gather | solution.py:52
  42.6 9.8 %gather_fusion.3 = f32[2048,64]{1,0:T(8,128)} fusion(f32[64,7552]{0,1:T(8,128)} %copy.24, s32[2048]{0:T(1024)S(1)} %get-tuple-element.138), kind=kCustom, calls=%fused_computation.1.clone | custom fusion | bytes 1056768 | tf_op jit(solution)/shard_map/jit(_take)/gather | solution.py:51
  52.4 0.0 copy-start.4
  52.4 0.0 copy-start.5
  52.5 4.4 %fusion.1 = f32[128,2048]{0,1:T(8,128)} fusion(f32[2048,128]{1,0:T(8,128)S(1)} %gather_fusion.2, f32[2048,128]{1,0:T(8,128)} %gather_fusion.1, f32[2048]{0:T(1024)S(1)} %get-tuple-element.135, f32[2048]{0:T(1024)S(1)} %get-tuple-element.136, pred[2048]{0:T(1024)(128)(4,1)S(1)} %get-tuple-element.134, pred[2048]{0:T(1024)(128)(4,1)S(1)} %get-tuple-element.137), kind=kLoop, calls=%fused_computation.13 | loop fusion | flops 1310720 | bytes 3166208 | tf_op jit(solution)/shard_map/sub | solution.py:51
  56.9 0.0 copy-done.4
  56.9 0.0 copy-done.5
  56.9 2.9 fusion
  59.8 46.7 %all-gather.2.cloned.1.call-done = f32[512,7552]{1,0:T(8,128)} async-done(((f32[16,7552]{1,0:T(8,128)}), f32[512,7552]{1,0:T(8,128)}) %all-gather.2.cloned.1.call-update) | async-done | bytes 15466512 | tf_op jit(solution)/shard_map/all_gather | solution.py:28
  106.5 0.0 copy-start.1
  106.5 0.0 copy-start.2
  106.5 19.0 %fusion.7 = f32[512,64]{0,1:T(8,128)S(1)} fusion(f32[512,7552]{1,0:T(8,128)} %all-gather.2.cloned.1.call-done, f32[64,7552]{1,0:T(8,128)S(1)} %copy-done.3), kind=kOutput, calls=%fused_computation.34 | convolution fusion | flops 2969567232 | bytes 17530880 | tf_op jit(solution)/shard_map/dot_general | solution.py:32
  125.5 0.0 copy-done.1
  125.5 0.0 copy-done.2
  125.5 0.0 copy-start.10
  125.5 0.0 copy-start.9
  125.6 16.4 %fusion.6 = f32[512,128]{0,1:T(8,128)S(1)} fusion(f32[512,7552]{1,0:T(8,128)S(1)} %copy-done.1, f32[128,7552]{1,0:T(8,128)S(1)} %copy-done.2), kind=kOutput, calls=%fused_computation.33 | convolution fusion | flops 5939134464 | bytes 19595264 | tf_op jit(solution)/shard_map/dot_general | solution.py:29
  142.0 0.8 pad_maximum_fusion
  142.8 0.0 all-reduce.4.cloned.1.call-update
  142.8 0.0 copy-done.10
  142.8 0.6 dynamic-slice
  144.1 0.0 copy-done.9
  144.2 125.6 %all-reduce.4.cloned.1.call-done = (f32[512,192]{0,1:T(8,128)}, f32[128,2048]{0,1:T(8,128)}, f32[64,2048]{0,1:T(8,128)}) async-done(((f32[512,192]{0,1:T(8,128)}, f32[128,2048]{0,1:T(8,128)}, f32[64,2048]{0,1:T(8,128)}), (f32[512,192]{0,1:T(8,128)}, f32[128,2048]{0,1:T(8,128)}, f32[64,2048]{0,1:T(8,128)})) %all-reduce.4.cloned.1.call-update) | async-done | bytes 1966096 | tf_op jit(solution)/shard_map/psum | solution.py:37
  269.8 0.0 copy-start.6
  269.8 1.0 fusion.5
  270.8 0.1 copy.26
  270.9 0.1 copy.27
  271.0 0.9 dynamic-slice.2
  271.8 38.4 %all_gather.10 = f32[64,2048]{0,1:T(8,128)S(1)} all-gather(f32[64,64]{0,1:T(8,128)S(1)} %dynamic-slice.2), channel_id=1, replica_groups=mesh['branch'=32,'bus'=8] {'branch'}, dimensions={1}, use_global_device_ids=true | all-gather | bytes 540672 | tf_op jit(solution)/shard_map/all_gather | solution.py:61
  310.3 0.3 copy.28
  310.6 0.8 constant_dynamic-slice_fusion.3
  311.3 0.8 gather_fusion
  312.2 0.3 dynamic-update-slice
  312.4 53.5 %all-reduce = f32[2048]{0:T(1024)S(1)} all-reduce(f32[2048]{0:T(1024)S(1)} %dynamic-update-slice), channel_id=1, replica_groups=mesh['branch'=32,'bus'=8] {'branch'}, use_global_device_ids=true, to_apply=%add | all-reduce | flops 2048 | bytes 16384
  365.9 0.0 copy-done.6
  365.9 0.3 divide_bitcast_fusion
  366.3 21.7 %while.13 = (s32[]{:T(128)}, f32[64,128]{1,0:T(8,128)S(1)}, f32[64,128]{1,0:T(8,128)S(1)}, f32[64,2048]{1,0:T(8,128)S(1)}, f32[2048,128]{1,0:T(8,128)S(1)}, /*index=5*/s32[]{:T(128)}, s32[]{:T(128)}, s32[]{:T(128)}, s32[]{:T(128)}) while((s32[]{:T(128)}, f32[64,128]{1,0:T(8,128)S(1)}, f32[64,128]{1,0:T(8,128)S(1)}, f32[64,2048]{1,0:T(8,128)S(1)}, ...), condition=%wide.region_5.8_spmd, body=%wide.region_3.7_spmd.sunk | while | flops 8388614 | bytes 753819 | solution.py:17
  366.3 2.6 abs_reduce_fusion.2
  369.1 2.6 abs_reduce_fusion.2
  371.8 2.6 abs_reduce_fusion.2
  374.5 2.6 abs_reduce_fusion.2
  377.2 2.6 abs_reduce_fusion.2
  379.9 2.6 abs_reduce_fusion.2
  382.6 2.6 abs_reduce_fusion.2
  385.4 2.6 abs_reduce_fusion.2
  388.0 0.0 copy-done
  388.0 0.8 convolution_divide_fusion
  (30 shorter events, 0.4 us)
Async XLA Ops:
  6.5 381.5 %copy-start = (f32[128,4]{0,1:T(4,128)S(1)}, f32[128,4]{0,1:T(4,128)}, u32[]{:S(2)}) copy-start(f32[128,4]{0,1:T(4,128)} %param.19) | copy-start | bytes 6148
  6.5 100.0 %all-gather.2.cloned.1.call-start = ((), (), s32[]{:S(2)}) async-start(), calls=%async_computation | async-start | bytes 15949824 | tf_op jit(solution)/shard_map/all_gather | solution.py:28
  7.3 262.5 %all-reduce.4.cloned.1.call-start = ((), (), s32[]{:S(2)}) async-start(), calls=%async_computation.1 | async-start | bytes 4980736 | tf_op jit(solution)/shard_map/psum | solution.py:37
  7.3 5.4 %copy-start.7 = (s32[2048]{0:T(1024)S(1)}, s32[2048]{0:T(1024)}, u32[]{:S(2)}) copy-start(s32[2048]{0:T(1024)} %param.16) | copy-start | bytes 24580
  7.3 5.4 %copy-start.8 = (s32[2048]{0:T(1024)S(1)}, s32[2048]{0:T(1024)}, u32[]{:S(2)}) copy-start(s32[2048]{0:T(1024)} %param.17) | copy-start | bytes 24580
  20.3 9.9 %copy-start.3 = (f32[64,7552]{1,0:T(8,128)S(1)}, f32[64,7552]{1,0:T(8,128)}, u32[]{:S(2)}) copy-start(f32[64,7552]{1,0:T(8,128)} %param.15) | copy-start | bytes 5799940
  52.4 4.5 %copy-start.4 = (f32[2048,64]{1,0:T(8,128)S(1)}, f32[2048,64]{1,0:T(8,128)}, u32[]{:S(2)}) copy-start(f32[2048,64]{1,0:T(8,128)} %gather_fusion.4) | copy-start | bytes 1572868
  52.4 4.5 %copy-start.5 = (f32[2048,64]{1,0:T(8,128)S(1)}, f32[2048,64]{1,0:T(8,128)}, u32[]{:S(2)}) copy-start(f32[2048,64]{1,0:T(8,128)} %gather_fusion.3) | copy-start | bytes 1572868
  106.5 19.0 %copy-start.1 = (f32[512,7552]{1,0:T(8,128)S(1)}, f32[512,7552]{1,0:T(8,128)}, u32[]{:S(2)}) copy-start(f32[512,7552]{1,0:T(8,128)} %all-gather.2.cloned.1.call-done) | copy-start | bytes 46399492
  106.5 19.0 %copy-start.2 = (f32[128,7552]{1,0:T(8,128)S(1)}, f32[128,7552]{1,0:T(8,128)}, u32[]{:S(2)}) copy-start(f32[128,7552]{1,0:T(8,128)} %param.14) | copy-start | bytes 11599876
  125.5 17.2 %copy-start.10 = (u32[256]{0:T(256)S(1)}, u32[256]{0:T(256)}, u32[]{:S(2)}) copy-start(u32[256]{0:T(256)} %constant.114) | copy-start | bytes 3076
  125.5 18.6 %copy-start.9 = (s32[64]{0:T(128)S(1)}, s32[64]{0:T(128)}, u32[]{:S(2)}) copy-start(s32[64]{0:T(128)} %param.18) | copy-start | bytes 772
  269.8 96.1 %copy-start.6 = (f32[128,2048]{0,1:T(8,128)S(1)}, f32[128,2048]{0,1:T(8,128)}, u32[]{:S(2)}) copy-start(f32[128,2048]{0,1:T(8,128)} %get-tuple-element.128) | copy-start | bytes 3145732
Sparse Core Ops, SparseCore 0:
  9.2 97.2 all-gather.1
  142.9 126.8 all-reduce.3
where the time goes:
time: 397 us; the launch traced here: 396 us
  waiting for transfers between devices  173 us (44%)
  blocking collectives  91.9 us (23%)
  local copies, waits for them, and re-layouts  49.2 us (12%)
  matrix products  36.2 us (9%)
  other arithmetic  30.6 us (8%)
  between operations  14.3 us (4%)
    psum x1, waiting for transfers between devices, on_device(): summed_flows = lax.psum(partial_flows, 'bus')  126 us
    unnamed x1, blocking collectives  53.5 us
    all_gather x1, waiting for transfers between devices, on_device(): piece = lax.all_gather(injections, 'branch', axis=0, tiled=True)  46.7 us
    all_gather x1, blocking collectives, on_device(): lax.all_gather(base_out, 'branch', axis=1, tiled=True)  38.4 us
    reduce_max x8, other arithmetic, advance(): return jnp.maximum(worst_load, jnp.max(jnp.abs(after_outage), axis=1))  21 us
    gather x2, local copies, waits for them, and re-layouts, columns(): jnp.take(matrix, from_index, axis=1) * from_inside[None, :]  19.6 us
    dot_general x1, matrix products, on_device(): lax.dot_general(piece, ptdf_out, contract, precision=highest, preferred_e...  19 us
    gather x2, local copies, waits for them, and re-layouts, columns(): jnp.take(matrix, to_index, axis=1) * to_inside[None, :]  17.3 us
  transfers between devices with their start and end apart: 2, of which 2 were waited for; matrix products, arithmetic and copies ran while one was open for 13% of the time, Pallas kernels for 0%

commit v1 on v0

v1 whole, which is shorter than its diff:
```python
import functools

import jax
import jax.numpy as jnp
from jax import lax
from jax.experimental import pallas as pl
from jax.experimental.pallas import tpu as pltpu
from jax.sharding import PartitionSpec as P

MESH = pl.DeviceIdType.MESH
F32 = jnp.float32
BF16 = jnp.bfloat16
NT = (((1,), (1,)), ((), ()))


def split_bf16(x):
    hi = x.astype(BF16)
    return hi, (x - hi.astype(F32)).astype(BF16)


def gather_kernel(
    inj, mon, out, ids_from, ids_to,
    flows, sens, self_out,
    a, b32, bhi, blo, frm, too, onehot,
    zs, zr, ys, yr, cs, cr, bsem,
):
    me = lax.axis_index("branch")
    bus = lax.axis_index("bus")
    width = mon.shape[1]
    mrows, orows = mon.shape[0], out.shape[0]
    z = me // 4
    y = (me // 2) % 2
    p = me % 2
    oy = 1 - y
    up = {"branch": (me + 4) % 32}
    down = {"branch": (me + 28) % 32}
    across = {"branch": z * 4 + oy * 2 + p}
    mate = {"branch": z * 4 + y * 2 + (1 - p)}

    load_b = [
        pltpu.make_async_copy(mon, b32.at[pl.ds(0, mrows)], bsem.at[0]),
        pltpu.make_async_copy(out, b32.at[pl.ds(mrows, orows)], bsem.at[1]),
    ]
    own_copy = [
        pltpu.make_async_copy(inj.at[pl.ds(8 * e, 8)], a.at[z, y, p, e], bsem.at[2 + e])
        for e in range(2)
    ]
    for c in load_b + own_copy:
        c.start()

    barrier = pltpu.get_barrier_semaphore()
    for d in (up, down, across, mate):
        pl.semaphore_signal(barrier, inc=1, device_id=d, device_id_type=MESH)
    pl.semaphore_wait(barrier, 4)

    def slot(delta):
        return (z + (delta + 8)) % 8

    def chunk(delta, yy, pp, e):
        return a.at[slot(delta), yy, pp, e]

    sends = []

    def send(src, dst, ssem, rsem, dev):
        c = pltpu.make_async_remote_copy(
            src_ref=src, dst_ref=dst, send_sem=ssem, recv_sem=rsem,
            device_id=dev, device_id_type=MESH,
        )
        c.start()
        sends.append(c)

    def arrived(ref, rsem):
        pltpu.make_async_remote_copy(
            src_ref=ref, dst_ref=ref, send_sem=rsem, recv_sem=rsem,
            device_id=mate, device_id_type=MESH,
        ).wait_recv()

    def send_z(direction, item):
        sign = 1 if direction == 0 else -1
        if item < 6:
            step, e, yy = item // 2 + 1, item % 2, y
        elif item == 6:
            step, e, yy = 4, direction, y
        else:
            step, e, yy = item - 6, 0, oy
        delta = -sign * (step - 1)
        dst = chunk(delta, yy, p, e)
        src = inj.at[pl.ds(8 * e, 8)] if item < 2 else dst
        send(src, dst, zs.at[direction, item], zr.at[direction, item], up if direction == 0 else down)

    def recv_z(direction, item):
        sign = 1 if direction == 0 else -1
        if item < 6:
            step, e, yy = item // 2 + 1, item % 2, y
        elif item == 6:
            step, e, yy = 4, direction, y
        else:
            step, e, yy = item - 6, 0, oy
        delta = -sign * step
        arrived(chunk(delta, yy, p, e), zr.at[direction, item])
        send_c(delta, yy, e)

    y_items = [(0, 0), (0, 1), (-1, 1), (1, 1), (-2, 1), (2, 1), (-3, 1), (3, 1), (-4, 0), (-4, 1)]

    def send_y(item):
        delta, e = y_items[item]
        dst = chunk(delta, y, p, e)
        src = inj.at[pl.ds(8 * e, 8)] if item < 2 else dst
        send(src, dst, ys.at[item], yr.at[item], across)

    def recv_y(item):
        delta, e = y_items[item]
        arrived(chunk(delta, oy, p, e), yr.at[item])
        send_c(delta, oy, e)

    c_items = []

    def send_c(delta, yy, e):
        item = len(c_items)
        other = 0 if yy is y else 1
        c_items.append((delta, other, e))
        dst = chunk(delta, yy, p, e)
        src = inj.at[pl.ds(8 * e, 8)] if (delta == 0 and other == 0) else dst
        send(src, dst, cs.at[item], cr.at[item], mate)

    got_c = set()

    def recv_c(deltas):
        for item, (delta, other, e) in enumerate(c_items):
            if delta in deltas and item not in got_c:
                got_c.add(item)
                arrived(chunk(delta, oy if other else y, 1 - p, e), cr.at[item])

    def block(delta):
        k = slot(delta)
        x = a[k].reshape(64, width)
        hi, lo = split_bf16(x)
        acc = lax.dot_general(hi, bhi[...], NT, preferred_element_type=F32)
        acc = acc + lax.dot_general(lo, bhi[...], NT, preferred_element_type=F32)
        acc = acc + lax.dot_general(hi, blo[...], NT, preferred_element_type=F32)
        flows[pl.ds(pl.multiple_of(k * 64, 64), 64)] = acc

    shift = bus * width

    def index_columns():
        f = ids_from[...] - shift
        t = ids_to[...] - shift
        same = f == t
        f = jnp.where(same, -1, f)
        t = jnp.where(same, -1, t)
        for i in range(f.shape[0]):
            frm[pl.ds(i * 128, 128)] = jnp.broadcast_to(f[i:i + 1], (128, 128)).T
            too[pl.ds(i * 128, 128)] = jnp.broadcast_to(t[i:i + 1], (128, 128)).T

    tiles = width // 128
    lane = lax.broadcasted_iota(jnp.int32, (1, 128), 1)

    def self_part():
        rows = pl.ds(pl.multiple_of(me * orows, orows), orows)
        f, t = frm[rows], too[rows]

        def step(j, acc):
            cols = pl.ds(pl.multiple_of(j * 128, 128), 128)
            v = b32[pl.ds(mrows, orows), cols]
            at = lane + j * 128
            return acc + jnp.where(f == at, v, 0.0) - jnp.where(t == at, v, 0.0)

        acc = lax.fori_loop(0, tiles, step, jnp.zeros((orows, 128), F32))
        self_out[...] = jnp.broadcast_to(jnp.sum(acc, axis=1, keepdims=True), (orows, 128))

    def sens_part(n):
        size = 256
        rows = pl.ds(n * size, size)

        def step(j, _):
            cols = pl.ds(pl.multiple_of(j * 128, 128), 128)
            at = lane + j * 128
            onehot[:, cols] = jnp.where(
                frm[rows] == at, 1.0, jnp.where(too[rows] == at, -1.0, 0.0)
            ).astype(BF16)
            return 0

        lax.fori_loop(0, tiles, step, 0)
        acc = lax.dot_general(bhi[pl.ds(0, mrows)], onehot[...], NT, preferred_element_type=F32)
        acc = acc + lax.dot_general(blo[pl.ds(0, mrows)], onehot[...], NT, preferred_element_type=F32)
        sens[:, rows] = acc

    for e in range(2):
        send_z(0, e)
        send_z(1, e)
        send_y(e)
        send_c(0, y, e)
    for c in load_b:
        c.wait()
    index_columns()
    for r in range(0, mrows + orows, 64):
        hi, lo = split_bf16(b32[pl.ds(r, 64)])
        bhi[pl.ds(r, 64)] = hi
        blo[pl.ds(r, 64)] = lo
    for c in own_copy:
        c.wait()

    both = (0, 1)
    for d in both:
        recv_z(d, 0)
        send_z(d, 2)
    recv_y(0)
    self_part()
    for d in both:
        recv_z(d, 1)
        send_z(d, 3)
    send_y(2), send_y(3)
    recv_y(1)
    for d in both:
        send_z(d, 7)
    sens_part(0)
    for d in both:
        recv_z(d, 2)
        send_z(d, 4)
    sens_part(1)
    for d in both:
        recv_z(d, 3)
        send_z(d, 5)
    send_y(4), send_y(5)
    recv_y(2), recv_y(3)
    for d in both:
        recv_z(d, 7)
        send_z(d, 8)
    sens_part(2)
    recv_z(0, 4)
    send_z(0, 6)
    recv_z(1, 4)
    sens_part(3)
    recv_z(0, 5)
    recv_z(1, 5)
    send_z(1, 6)
    send_y(6), send_y(7)
    recv_y(4), recv_y(5)
    for d in both:
        recv_z(d, 8)
        send_z(d, 9)
    for n in range(4, 8):
        sens_part(n)
    recv_c((0, 1, -1))
    recv_z(0, 6)
    send_y(8)
    recv_z(1, 6)
    send_y(9)
    block(0)
    block(1)
    block(-1)
    recv_y(6), recv_y(7)
    recv_c((2, -2))
    block(2)
    block(-2)
    for d in both:
        recv_z(d, 9)
    recv_y(8), recv_y(9)
    recv_c((3, -3, 4, -4))
    block(3)
    block(-3)
    block(-4)
    for c in sends:
        c.wait_send()


def gather_flows(injections, ptdf_mon, ptdf_out, outage_from, outage_to):
    mrows, width = ptdf_mon.shape
    orows = ptdf_out.shape[0]
    outages = outage_from.shape[0]
    hours = injections.shape[0] * lax.axis_size("branch")
    rows = mrows + orows
    hbm = pl.BlockSpec(memory_space=pl.ANY)
    vmem = pl.BlockSpec(memory_space=pltpu.VMEM)
    dma = pltpu.SemaphoreType.DMA
    return pl.pallas_call(
        gather_kernel,
        out_shape=(
            jax.ShapeDtypeStruct((hours, rows), F32),
            jax.ShapeDtypeStruct((mrows, outages), F32),
            jax.ShapeDtypeStruct((orows, 128), F32),
        ),
        in_specs=[hbm, hbm, hbm, vmem, vmem],
        out_specs=(vmem, vmem, vmem),
        scratch_shapes=[
            pltpu.VMEM((8, 2, 2, 2, 8, width), F32),
            pltpu.VMEM((rows, width), F32),
            pltpu.VMEM((rows, width), BF16),
            pltpu.VMEM((rows, width), BF16),
            pltpu.VMEM((outages, 128), jnp.int32),
            pltpu.VMEM((outages, 128), jnp.int32),
            pltpu.VMEM((256, width), BF16),
            dma((2, 10)), dma((2, 10)), dma((10,)), dma((10,)), dma((32,)), dma((32,)), dma((4,)),
        ],
        compiler_params=pltpu.CompilerParams(
            collective_id=0, has_side_effects=True, vmem_limit_bytes=64 * 1024 * 1024 - 128 * 1024
        ),
        name="gather_flows",
    )(injections, ptdf_mon, ptdf_out, outage_from.reshape(-1, 128), outage_to.reshape(-1, 128))


def screen(base_mon, outage_base, lodf_t, block_size):
    outage_count = lodf_t.shape[0]

    def advance(index, worst_load):
        first = index * block_size
        lodf_block = lax.dynamic_slice_in_dim(lodf_t, first, block_size, 0)
        flow_block = lax.dynamic_slice_in_dim(outage_base, first, block_size, 1)
        after_outage = base_mon[:, None, :] + flow_block[:, :, None] * lodf_block[None, :, :]
        return jnp.maximum(worst_load, jnp.max(jnp.abs(after_outage), axis=1))

    return lax.fori_loop(0, outage_count // block_size, advance, jnp.abs(base_mon))


def on_device(injections, ptdf_mon, ptdf_out, outage_from, outage_to, hour_ids, ratings):
    highest = lax.Precision.HIGHEST
    mon_rows = ptdf_mon.shape[0]
    bus_count = lax.axis_size("bus")
    bus_index = lax.axis_index("bus")
    partial_flows, sens_part, self_part = gather_flows(
        injections, ptdf_mon, ptdf_out, outage_from, outage_to
    )
    hours_dev = partial_flows.shape[0] // bus_count
    summed_flows, sens_mon, self_sens = lax.psum((partial_flows, sens_part, self_part[:, 0]), "bus")
    base_flows = lax.dynamic_slice_in_dim(summed_flows, bus_index * hours_dev, hours_dev, 0)
    base_mon = base_flows[:, :mon_rows]
    base_out = base_flows[:, mon_rows:]
    outage_base, outage_self = (
        lax.all_gather(base_out, "branch", axis=1, tiled=True),
        lax.all_gather(self_sens, "branch", axis=0, tiled=True),
    )
    divisor = jnp.maximum(1.0 - outage_self, 0.25)
    lodf_t = (sens_mon / divisor[None, :]).T
    worst_load = screen(base_mon, outage_base, lodf_t, min(256, lodf_t.shape[0]))
    season = hour_ids * 4 // 8760
    onehot = (season[:, None] == jnp.arange(ratings.shape[1], dtype=jnp.int32)[None, :]).astype(
        jnp.float32
    )
    hour_rating = jnp.dot(onehot, ratings.T, precision=highest, preferred_element_type=jnp.float32)
    return worst_load / hour_rating


def solution(mesh):
    placed = (
        P("branch", "bus"),
        P("branch", "bus"),
        P("branch", "bus"),
        P(),
        P(),
        P("bus"),
        P("branch", None),
    )
    return jax.shard_map(
        on_device, mesh=mesh, in_specs=placed, out_specs=P("bus", "branch"), check_vma=False
    )
```

time: 397 us -> 285 us (0.72)
  waiting for transfers between devices: 173 us -> 18.4 us
  Pallas kernels: 0 us -> 107 us
  local copies, waits for them, and re-layouts: 49.2 us -> 3.91 us
  matrix products: 36.2 us -> 0.83 us
  blocking collectives: 91.9 us -> 117 us
  other arithmetic: 30.6 us -> 23.1 us
    psum x1, waiting for transfers between devices: 126 us -> 18.4 us  [on_device(): lax.psum((partial_flows, sens_part, self_part[:, 0]), 'bus')]
    pallas_call x0 -> x1, Pallas kernels: none -> 107 us  [gather_flows(): pl.pallas_call(gather_kernel, out_shape=(jax.ShapeDtypeStruct((hours, row...]
    all_gather x1 -> x0, waiting for transfers between devices: 46.7 us -> none  [on_device(): piece = lax.all_gather(injections, 'branch', axis=0, tiled=True)]
    gather x5 -> x0, local copies, waits for them, and re-layouts: 37.8 us -> none  [the longest x2 19.6 us: columns(): jnp.take(matrix, from_index, axis=1) * from_inside[None, :]]
    dot_general x2 -> x0, matrix products: 35.4 us -> none  [the longest x1 19 us: on_device(): lax.dot_general(piece, ptdf_out, contract, precision=highest, preferred_e...]
    psum x0 -> x1, blocking collectives: none -> 20.3 us  [on_device(): lax.psum((partial_flows, sens_part, self_part[:, 0]), 'bus')]
    unnamed x27 -> x9, local copies, waits for them, and re-layouts: 9.07 us -> 0.95 us
    sub x2 -> x0, other arithmetic: 7.3 us -> none  [columns(): jnp.take(matrix, from_index, axis=1) * from_inside[None, :]]
  transfers between devices with their start and end apart: 2 -> 1, of which waited for: 2 -> 1; matrix products, arithmetic and copies ran while one was open for 13% -> 1% of each run, Pallas kernels for 0% -> 0%
where the time goes in v1:
time: 285 us
  blocking collectives  117 us (41%)
  Pallas kernels  107 us (38%)
  other arithmetic  23.1 us (8%)
  waiting for transfers between devices  18.4 us (6%)
  between operations  14.2 us (5%)
  local copies, waits for them, and re-layouts  3.91 us (1%)
    pallas_call x1, Pallas kernels, gather_flows(): pl.pallas_call(gather_kernel, out_shape=(jax.ShapeDtypeStruct((hours, row...  107 us
    unnamed x1, blocking collectives  56.5 us
    all_gather x1, blocking collectives, on_device(): lax.all_gather(base_out, 'branch', axis=1, tiled=True)  40.1 us
    reduce_max x8, other arithmetic, advance(): return jnp.maximum(worst_load, jnp.max(jnp.abs(after_outage), axis=1))  21 us
    psum x1, blocking collectives, on_device(): lax.psum((partial_flows, sens_part, self_part[:, 0]), 'bus')  20.3 us
    psum x1, waiting for transfers between devices, on_device(): lax.psum((partial_flows, sens_part, self_part[:, 0]), 'bus')  18.4 us
  transfers between devices with their start and end apart: 1, of which 1 were waited for; matrix products, arithmetic and copies ran while one was open for 1% of the time, Pallas kernels for 0%

profile of v1, /device:TPU:1, one launch (start us, length us, event | category | flops | bytes accessed | tf_op | source)
XLA Modules:
  0.0 284.9 jit_solution(16759614128814126783)
XLA Ops:
  6.5 0.0 copy-start
  6.5 0.0 all-reduce.4.cloned.1.call-start
  6.5 0.0 copy-start.2
  6.5 0.0 copy-start.1
  6.5 107.0 %gather_flows.1 = (f32[512,192]{1,0:T(8,128)}, f32[128,2048]{1,0:T(8,128)}, f32[64,128]{1,0:T(8,128)}) custom-call(f32[16,7552]{1,0:T(8,128)} %inj.1, f32[128,7552]{1,0:T(8,128)} %mon.1, f32[64,7552]{1,0:T(8,128)} %out.1, s32[16,128]{1,0:T(8,128)} %bitcast.6, s32[16,128]{1,0:T(8,128)} %bitcast.7), custom_call_target="tpu_custom_call" | custom-call | tf_op jit(solution)/shard_map/gather_flows/pallas_call | solution.py:276
  113.6 0.0 all-reduce.4.cloned.1.call-update
  113.6 0.0 copy-done.2
  113.6 0.7 dynamic-slice
  115.0 0.9 slice_reduce_fusion
  115.8 20.3 %psum.23 = f32[64]{0:T(128)S(1)} all-reduce(f32[64]{0:T(128)S(1)} %slice_reduce_fusion), channel_id=1, replica_groups=mesh['branch'=32,'bus'=8] {'bus'}, use_global_device_ids=true, to_apply=%region_2.0 | all-reduce | flops 64 | bytes 512 | tf_op jit(solution)/shard_map/psum | solution.py:324
  136.1 0.3 dynamic-update-slice
  136.4 56.5 %all-reduce = f32[2048]{0:T(1024)S(1)} all-reduce(f32[2048]{0:T(1024)S(1)} %dynamic-update-slice), channel_id=1, replica_groups=mesh['branch'=32,'bus'=8] {'branch'}, use_global_device_ids=true, to_apply=%add | all-reduce | flops 2048 | bytes 16384
  192.9 0.0 copy-done.1
  192.9 18.4 %all-reduce.4.cloned.1.call-done = (f32[512,192]{1,0:T(8,128)}, f32[128,2048]{1,0:T(8,128)}) async-done(((f32[512,192]{1,0:T(8,128)}, f32[128,2048]{1,0:T(8,128)}), (f32[512,192]{1,0:T(8,128)}, f32[128,2048]{1,0:T(8,128)})) %all-reduce.4.cloned.1.call-update) | async-done | bytes 1441808 | tf_op jit(solution)/shard_map/psum | solution.py:324
  211.3 0.8 fusion.1
  212.1 0.8 dynamic-slice.2
  212.9 0.1 copy.13
  212.9 40.1 %all_gather.6 = f32[64,2048]{0,1:T(8,128)S(1)} all-gather(f32[64,64]{0,1:T(8,128)S(1)} %copy.13), channel_id=1, replica_groups=mesh['branch'=32,'bus'=8] {'branch'}, dimensions={1}, use_global_device_ids=true | all-gather | bytes 540672 | tf_op jit(solution)/shard_map/all_gather | solution.py:329
  253.1 0.3 copy.14
  253.4 1.3 divide_bitcast_fusion
  254.7 22.4 %while.13 = (s32[]{:T(128)}, f32[64,128]{1,0:T(8,128)S(1)}, f32[64,128]{1,0:T(8,128)S(1)}, f32[64,2048]{1,0:T(8,128)S(1)}, f32[2048,128]{0,1:T(8,128)S(1)}, /*index=5*/s32[]{:T(128)}, s32[]{:T(128)}, s32[]{:T(128)}, s32[]{:T(128)}) while((s32[]{:T(128)}, f32[64,128]{1,0:T(8,128)S(1)}, f32[64,128]{1,0:T(8,128)S(1)}, f32[64,2048]{1,0:T(8,128)S(1)}, ...), condition=%wide.region_5.0_spmd, body=%wide.region_3.0_spmd.sunk | while | flops 8388614 | bytes 1015963 | solution.py:312
  254.8 0.1 copy.18
  254.9 2.6 abs_reduce_fusion.2
  257.6 0.1 copy.18
  257.7 2.6 abs_reduce_fusion.2
  260.4 0.1 copy.18
  260.5 2.6 abs_reduce_fusion.2
  263.2 0.1 copy.18
  263.3 2.6 abs_reduce_fusion.2
  266.0 0.1 copy.18
  266.1 2.6 abs_reduce_fusion.2
  268.8 0.1 copy.18
  268.9 2.6 abs_reduce_fusion.2
  271.6 0.1 copy.18
  271.7 2.6 abs_reduce_fusion.2
  274.4 0.1 copy.18
  274.5 2.6 abs_reduce_fusion.2
  277.2 0.0 copy-done
  277.2 0.8 convolution_divide_fusion
  (27 shorter events, 0.3 us)
Async XLA Ops:
  6.5 270.7 %copy-start = (f32[128,4]{0,1:T(4,128)S(1)}, f32[128,4]{0,1:T(4,128)}, u32[]{:S(2)}) copy-start(f32[128,4]{0,1:T(4,128)} %param.15) | copy-start | bytes 6148
  6.5 204.8 %all-reduce.4.cloned.1.call-start = ((), (), s32[]{:S(2)}) async-start(), calls=%async_computation | async-start | bytes 3145728 | tf_op jit(solution)/shard_map/psum | solution.py:324
  6.5 107.0 %copy-start.2 = (u32[256]{0:T(256)S(1)}, u32[256]{0:T(256)}, u32[]{:S(2)}) copy-start(u32[256]{0:T(256)} %constant.63) | copy-start | bytes 3076
  6.5 186.3 %copy-start.1 = (s32[64]{0:T(128)S(1)}, s32[64]{0:T(128)}, u32[]{:S(2)}) copy-start(s32[64]{0:T(128)} %param.14) | copy-start | bytes 772
Sparse Core Ops, SparseCore 0:
  113.7 97.5 all-reduce.3

commit v2 on v1

v2 whole, which is shorter than its diff:
```python
import functools

import jax
import jax.numpy as jnp
from jax import lax
from jax.experimental import pallas as pl
from jax.experimental.pallas import tpu as pltpu
from jax.sharding import PartitionSpec as P

MESH = pl.DeviceIdType.MESH
F32 = jnp.float32
BF16 = jnp.bfloat16
NT = (((1,), (1,)), ((), ()))


def split_bf16(x):
    hi = x.astype(BF16)
    return hi, (x - hi.astype(F32)).astype(BF16)


def screen_kernel(
    inj, mon, out, ids_from, ids_to, hour_ids, ratings,
    result,
    a, b32, bl, bthi, btlo, onehot, ahi, alo,
    part, parts3, tot, qsum, lod, send_flow, recv_flow, packs, fscr,
    zs, zr, ys, yr, cs, cr, bsem, xs, xr, fs, fr, pzs, pzr, pys, pyr, pcs, pcr,
):
    me = lax.axis_index("branch")
    bus = lax.axis_index("bus")
    width = mon.shape[1]
    mrows, orows = mon.shape[0], out.shape[0]
    z = me // 4
    y = (me // 2) % 2
    p = me % 2
    oy = 1 - y
    x = bus // 2
    h = bus % 2
    up = {"branch": (me + 4) % 32}
    down = {"branch": (me + 28) % 32}
    across = {"branch": z * 4 + oy * 2 + p}
    mate = {"branch": z * 4 + y * 2 + (1 - p)}

    load_b = [
        pltpu.make_async_copy(mon, b32.at[pl.ds(0, mrows)], bsem.at[0]),
        pltpu.make_async_copy(out, b32.at[pl.ds(mrows, orows)], bsem.at[1]),
    ]
    own_copy = [
        pltpu.make_async_copy(inj.at[pl.ds(8 * e, 8)], a.at[z, y, p, e], bsem.at[2 + e])
        for e in range(2)
    ]
    for c in load_b + own_copy:
        c.start()

    barrier = pltpu.get_barrier_semaphore()
    peers = [across, mate]
    peers += [{"branch": (me + 4 * k) % 32} for k in range(1, 8)]
    peers += [{"bus": (bus + k) % 8} for k in range(1, 8)]
    for d in peers:
        pl.semaphore_signal(barrier, inc=1, device_id=d, device_id_type=MESH)
    pl.semaphore_wait(barrier, len(peers))

    def slot(delta):
        return (z + (delta + 8)) % 8

    def chunk(delta, yy, pp, e):
        return a.at[slot(delta), yy, pp, e]

    sends = []

    def send(src, dst, ssem, rsem, dev):
        c = pltpu.make_async_remote_copy(
            src_ref=src, dst_ref=dst, send_sem=ssem, recv_sem=rsem,
            device_id=dev, device_id_type=MESH,
        )
        c.start()
        sends.append(c)

    def arrived(ref, rsem):
        pltpu.make_async_remote_copy(
            src_ref=ref, dst_ref=ref, send_sem=rsem, recv_sem=rsem,
            device_id=mate, device_id_type=MESH,
        ).wait_recv()

    def z_item(direction, item):
        if item < 6:
            return item // 2 + 1, item % 2, y
        if item == 6:
            return 4, direction, y
        return item - 6, 0, oy

    def send_z(direction, item):
        sign = 1 if direction == 0 else -1
        step, e, yy = z_item(direction, item)
        dst = chunk(-sign * (step - 1), yy, p, e)
        src = inj.at[pl.ds(8 * e, 8)] if item < 2 else dst
        send(src, dst, zs.at[direction, item], zr.at[direction, item], up if direction == 0 else down)

    def recv_z(direction, item):
        sign = 1 if direction == 0 else -1
        step, e, yy = z_item(direction, item)
        delta = -sign * step
        arrived(chunk(delta, yy, p, e), zr.at[direction, item])
        return lambda: send_c(delta, yy, e)

    y_items = [(0, 0), (0, 1), (-1, 1), (1, 1), (-2, 1), (2, 1), (-3, 1), (3, 1), (-4, 0), (-4, 1)]

    def send_y(item):
        delta, e = y_items[item]
        dst = chunk(delta, y, p, e)
        src = inj.at[pl.ds(8 * e, 8)] if item < 2 else dst
        send(src, dst, ys.at[item], yr.at[item], across)

    def recv_y(item):
        delta, e = y_items[item]
        arrived(chunk(delta, oy, p, e), yr.at[item])
        return lambda: send_c(delta, oy, e)

    c_items = []

    def send_c(delta, yy, e):
        item = len(c_items)
        other = 0 if yy is y else 1
        c_items.append((delta, other, e))
        dst = chunk(delta, yy, p, e)
        src = inj.at[pl.ds(8 * e, 8)] if (delta == 0 and other == 0) else dst
        send(src, dst, cs.at[item], cr.at[item], mate)

    got_c = set()

    def recv_c(deltas):
        for item, (delta, other, e) in enumerate(c_items):
            if delta in deltas and item not in got_c:
                got_c.add(item)
                arrived(chunk(delta, oy if other else y, 1 - p, e), cr.at[item])

    tiles = width // 128

    def block(deltas):
        rows = 64 * len(deltas)
        for n, delta in enumerate(deltas):
            hi, lo = split_bf16(a[slot(delta)].reshape(64, width))
            ahi[pl.ds(64 * n, 64)] = hi
            alo[pl.ds(64 * n, 64)] = lo
        top = pl.ds(0, rows)
        acc = jnp.dot(ahi[top], bthi[...], preferred_element_type=F32)
        acc = acc + jnp.dot(alo[top], bthi[...], preferred_element_type=F32)
        acc = acc + jnp.dot(ahi[top], btlo[...], preferred_element_type=F32)
        for n, delta in enumerate(deltas):
            k = slot(delta)
            got = acc[64 * n:64 * n + 64]
            send_flow[k, pl.ds(0, 64)] = got[:, :mrows]
            tail = got[:, mrows:]
            send_flow[k, pl.ds(64, 32)] = jnp.concatenate([tail[:32], tail[32:]], axis=1)

    shift = bus * width

    def transposed_b():
        def step(j, _):
            cols = pl.ds(pl.multiple_of(j * 128, 128), 128)
            for r, n in ((0, mrows), (mrows, orows)):
                hi, lo = split_bf16(b32[pl.ds(r, n), cols].T)
                bthi[cols, pl.ds(r, n)] = hi
                btlo[cols, pl.ds(r, n)] = lo
            return 0

        lax.fori_loop(0, tiles, step, 0)

    def left_b():
        for r in range(0, mrows, 32):
            hi, lo = split_bf16(b32[pl.ds(r, 32)])
            bl[pl.ds(r, 32)] = hi
            bl[pl.ds(mrows + r, 32)] = lo

    def index_rows(start, size):
        cols = pl.ds(pl.multiple_of(start, 128), size)
        f = ids_from[:, cols] - shift
        t = ids_to[:, cols] - shift
        same = f == t
        return jnp.where(same, -1, f), jnp.where(same, -1, t)

    def self_part():
        chip = me // 2
        f, t = index_rows(chip * 128, 128)
        f = jnp.broadcast_to(f, (128, 128)).T
        t = jnp.broadcast_to(t, (128, 128)).T
        mine = p == 0
        f = jnp.where(mine, f[:orows], f[orows:])
        t = jnp.where(mine, t[:orows], t[orows:])
        lane = lax.broadcasted_iota(jnp.int32, (1, 128), 1)

        def step(j, acc):
            cols = pl.ds(pl.multiple_of(j * 128, 128), 128)
            v = b32[pl.ds(mrows, orows), cols]
            at = lane + j * 128
            return acc + jnp.where(f == at, v, 0.0) - jnp.where(t == at, v, 0.0)

        acc = lax.fori_loop(0, tiles, step, jnp.zeros((orows, 128), F32))
        acc = jnp.concatenate([acc, jnp.zeros((128 - orows, 128), F32)], axis=0)
        row = jnp.sum(acc.T, axis=0, keepdims=True)
        for k in range(8):
            send_flow[k, pl.ds(96, 8)] = jnp.broadcast_to(row, (8, 128))

    def sens_part(d, half):
        i = (x + d) % 4
        f, t = index_rows(i * 512 + half * 256, 256)
        sub = lax.broadcasted_iota(jnp.int32, (128, 256), 0)

        def step(j, _):
            at = sub + j * 128
            onehot[pl.ds(pl.multiple_of(j * 128, 128), 128)] = jnp.where(
                f == at, 1.0, jnp.where(t == at, -1.0, 0.0)
            ).astype(BF16)
            return 0

        lax.fori_loop(0, tiles, step, 0)
        acc = jnp.dot(bl[...], onehot[...], preferred_element_type=F32)
        part[i, :, pl.ds(half * 256, 256)] = acc[:mrows] + acc[mrows:]

    def x_dev(d):
        return {"bus": ((x + d) % 4) * 2 + h}

    def send_part(d):
        send(part.at[(x + d) % 4], parts3.at[d - 1], xs.at[d - 1], xr.at[d - 1], x_dev(d))

    def sum_part():
        for d in (1, 2, 3):
            arrived(parts3.at[d - 1], xr.at[d - 1])
        tot[...] = part[x] + parts3[0] + parts3[1] + parts3[2]
        send(tot, qsum, xs.at[3], xr.at[3], {"bus": x * 2 + (1 - h)})

    def share_part():
        arrived(qsum, xr.at[3])
        sends[pair_send[0]].wait_send()
        lod[x] = tot[...] + qsum[...]
        for d in (1, 2, 3):
            send(lod.at[x], lod.at[x], xs.at[3 + d], xr.at[3 + d], x_dev(d))

    def take_part():
        for d in (1, 2, 3):
            arrived(lod.at[(x + 4 - d) % 4], xr.at[3 + d])

    pair_send = []

    def both(f, *items):
        for item in items:
            for d in (0, 1):
                f(d, item)

    def recv_both(item):
        return [recv_z(0, item), recv_z(1, item)]

    def run(fs_):
        for f_ in fs_:
            f_()

    for e in range(2):
        send_z(0, e)
        send_z(1, e)
        send_y(e)
        send_c(0, y, e)
    for c in load_b:
        c.wait()
    left_b()
    for c in own_copy:
        c.wait()
    sens_part(2, 0)
    q = recv_both(0)
    both(send_z, 2)
    q += [recv_y(0)]
    run(q)
    sens_part(2, 1)
    send_part(2)
    q = recv_both(1)
    both(send_z, 3)
    send_y(2), send_y(3)
    q += [recv_y(1)]
    both(send_z, 7)
    run(q)
    sens_part(1, 0)
    sens_part(1, 1)
    send_part(1)
    q = recv_both(2)
    both(send_z, 4)
    run(q)
    sens_part(3, 0)
    sens_part(3, 1)
    send_part(3)
    q = recv_both(3)
    both(send_z, 5)
    send_y(4), send_y(5)
    q += [recv_y(2), recv_y(3)]
    run(q)
    sens_part(0, 0)
    q = recv_both(7)
    both(send_z, 8)
    run(q)
    sens_part(0, 1)
    sum_part()
    pair_send.append(len(sends) - 1)
    q = [recv_z(0, 4)]
    send_z(0, 6)
    q += [recv_z(1, 4)]
    run(q)
    self_part()
    transposed_b()
    share_part()
    q = recv_both(5)
    send_z(1, 6)
    send_y(6), send_y(7)
    q += [recv_y(4), recv_y(5)]
    run(q)
    q = recv_both(8)
    both(send_z, 9)
    run(q)
    recv_c((0, 1, -1))
    block((0,))
    q = [recv_z(0, 6)]
    send_y(8)
    q += [recv_z(1, 6)]
    send_y(9)
    run(q)
    block((1, -1))
    run([recv_y(6), recv_y(7)])
    recv_c((2, -2))
    block((2, -2))
    run(recv_both(9) + [recv_y(8), recv_y(9)])
    recv_c((3, -3, 4, -4))
    block((3, -3, -4))

    for k in range(1, 8):
        to = (bus + k) % 8
        send(send_flow.at[to], recv_flow.at[k], fs.at[k], fr.at[k], {"bus": to})
    own = send_flow[bus]
    for k in range(1, 8):
        arrived(recv_flow.at[k], fr.at[k])
        own = own + recv_flow[k]
    recv_flow[0] = own
    packs[z, y, p] = recv_flow[0, pl.ds(64, 40)]

    def pack_to_y(k, zz):
        send(packs.at[zz, y, p], packs.at[zz, y, p], pys.at[k], pyr.at[k], across)

    def pack_to_c(k, zz, yy):
        send(packs.at[zz, yy, p], packs.at[zz, yy, p], pcs.at[k], pcr.at[k], mate)

    for k in (4, 3, 5, 2, 6, 1, 7):
        send(packs.at[z, y, p], packs.at[z, y, p], pzs.at[k], pzr.at[k], {"branch": (me + 4 * k) % 32})
    pack_to_y(0, z)
    pack_to_c(0, z, y)
    order = (1, 7, 2, 6, 3, 5, 4)
    for k in order:
        zz = (z + 8 - k) % 8
        arrived(packs.at[zz, y, p], pzr.at[k])
        pack_to_y(k, zz)
        pack_to_c(k, zz, y)
    for k in (0,) + order:
        zz = (z + 8 - k) % 8
        arrived(packs.at[zz, oy, p], pyr.at[k])
        pack_to_c(8 + k, zz, oy)
    for k in (0,) + order:
        zz = (z + 8 - k) % 8
        arrived(packs.at[zz, y, 1 - p], pcr.at[k])
        arrived(packs.at[zz, oy, 1 - p], pcr.at[8 + k])
    take_part()

    low = lax.broadcasted_iota(jnp.int32, (1, 128), 1) < 64

    def unpack(n, _):
        zz, yy = n // 2, n % 2
        p0, p1 = packs[zz, yy, 0], packs[zz, yy, 1]
        r0, r1 = pltpu.roll(p0, 64, 1), pltpu.roll(p1, 64, 1)
        first = jnp.where(low, p0, r1)
        second = jnp.where(low, r0, p1)
        scale = 1.0 / jnp.maximum(1.0 - first[32:33], 0.25)
        fscr[n, pl.ds(0, 32)] = first[:32] * scale
        fscr[n, pl.ds(32, 32)] = second[:32] * scale
        return 0

    lax.fori_loop(0, 16, unpack, 0)

    lane = lax.broadcasted_iota(jnp.int32, (1, 1, 128), 2)
    hb, mt = 4, 4

    def screen_m(g, _):
        rows = pl.ds(pl.multiple_of(g * (8 * mt), 8 * mt), 8 * mt)

        def screen_h(n, carry):
            top, bot = carry
            hi = [jnp.zeros((mt, 8, 128), F32) for _ in range(hb)]
            lo = [jnp.zeros((mt, 8, 128), F32) for _ in range(hb)]
            for kb in range(16):
                l = lod[kb // 4, rows, pl.ds((kb % 4) * 128, 128)].reshape(mt, 8, 128)
                for i in range(hb):
                    f = fscr[kb, pl.ds(n * hb + i, 8, stride=0)]
                    v = l * f[None]
                    hi[i] = jnp.maximum(hi[i], v)
                    lo[i] = jnp.minimum(lo[i], v)
            for i in range(hb):
                here = lane == n * hb + i
                top = jnp.where(here, jnp.max(hi[i], axis=2, keepdims=True), top)
                bot = jnp.where(here, jnp.min(lo[i], axis=2, keepdims=True), bot)
            return top, bot

        zero = jnp.zeros((mt, 8, 128), F32)
        top, bot = lax.fori_loop(0, 64 // hb, screen_h, (zero, zero))
        parts3[0, rows, pl.ds(0, 128)] = top.reshape(8 * mt, 128)
        parts3[1, rows, pl.ds(0, 128)] = bot.reshape(8 * mt, 128)
        return 0

    lax.fori_loop(0, mrows // (8 * mt), screen_m, 0)
    base = jnp.concatenate([recv_flow[0, pl.ds(0, 64)], jnp.zeros((64, 128), F32)], axis=0).T
    worst = jnp.maximum(
        jnp.abs(base + parts3[0, :, pl.ds(0, 128)]), jnp.abs(base + parts3[1, :, pl.ds(0, 128)])
    )
    hour = jnp.concatenate([hour_ids[...], jnp.zeros((1, 64), jnp.int32)], axis=1)
    season = (hour * 4) // 8760
    rating = jnp.where(season == 0, ratings[:, 0:1], ratings[:, 1:2])
    rating = jnp.where(season == 2, ratings[:, 2:3], rating)
    rating = jnp.where(season == 3, ratings[:, 3:4], rating)
    result[...] = (worst / rating).T[:64]
    done = set(pair_send)
    for n, c in enumerate(sends):
        if n not in done:
            c.wait_send()


def on_device(injections, ptdf_mon, ptdf_out, outage_from, outage_to, hour_ids, ratings):
    mrows, width = ptdf_mon.shape
    orows = ptdf_out.shape[0]
    rows = mrows + orows
    hbm = pl.BlockSpec(memory_space=pl.ANY)
    vmem = pl.BlockSpec(memory_space=pltpu.VMEM)
    dma = pltpu.SemaphoreType.DMA
    v = pltpu.VMEM
    return pl.pallas_call(
        screen_kernel,
        out_shape=jax.ShapeDtypeStruct((64, mrows), F32),
        in_specs=[hbm, hbm, hbm, vmem, vmem, vmem, vmem],
        out_specs=vmem,
        scratch_shapes=[
            v((8, 2, 2, 2, 8, width), F32),
            v((rows, width), F32),
            v((2 * mrows, width), BF16),
            v((width, rows), BF16),
            v((width, rows), BF16),
            v((width, 256), BF16),
            v((192, width), BF16),
            v((192, width), BF16),
            v((4, mrows, 512), F32),
            v((3, mrows, 512), F32),
            v((mrows, 512), F32),
            v((mrows, 512), F32),
            v((4, mrows, 512), F32),
            v((8, 104, 128), F32),
            v((8, 104, 128), F32),
            v((8, 2, 2, 40, 128), F32),
            v((16, 64, 128), F32),
            dma((2, 10)), dma((2, 10)), dma((10,)), dma((10,)), dma((32,)), dma((32,)), dma((4,)),
            dma((7,)), dma((7,)), dma((8,)), dma((8,)), dma((8,)), dma((8,)), dma((8,)), dma((8,)),
            dma((16,)), dma((16,)),
        ],
        compiler_params=pltpu.CompilerParams(
            collective_id=0, has_side_effects=True, vmem_limit_bytes=64 * 1024 * 1024 - 128 * 1024
        ),
        name="screen",
    )(
        injections, ptdf_mon, ptdf_out, outage_from.reshape(1, -1), outage_to.reshape(1, -1),
        hour_ids.reshape(1, -1), ratings,
    )


def solution(mesh):
    placed = (
        P("branch", "bus"),
        P("branch", "bus"),
        P("branch", "bus"),
        P(),
        P(),
        P("bus"),
        P("branch", None),
    )
    return jax.shard_map(
        on_device, mesh=mesh, in_specs=placed, out_specs=P("bus", "branch"), check_vma=False
    )
```

time: 285 us -> 120 us (0.42)
  blocking collectives: 117 us -> 0 us
  other arithmetic: 23.1 us -> 0 us
  waiting for transfers between devices: 18.4 us -> 0 us
  between operations: 14.2 us -> 0.01 us
  Pallas kernels: 107 us -> 116 us
    unnamed x1 -> x0, blocking collectives: 56.5 us -> none
    all_gather x1 -> x0, blocking collectives: 40.1 us -> none  [on_device(): lax.all_gather(base_out, 'branch', axis=1, tiled=True)]
    reduce_max x8 -> x0, other arithmetic: 21 us -> none  [advance(): return jnp.maximum(worst_load, jnp.max(jnp.abs(after_outage), axis=1))]
    psum x1 -> x0, blocking collectives: 20.3 us -> none  [on_device(): lax.psum((partial_flows, sens_part, self_part[:, 0]), 'bus')]
    psum x1 -> x0, waiting for transfers between devices: 18.4 us -> none  [on_device(): lax.psum((partial_flows, sens_part, self_part[:, 0]), 'bus')]
    pallas_call x1, Pallas kernels: 107 us -> 116 us  [on_device(): pl.pallas_call(screen_kernel, out_shape=jax.ShapeDtypeStruct((64, mrows),...]
  transfers between devices with their start and end apart: 1 -> 0, of which waited for: 1 -> 0; matrix products, arithmetic and copies ran while one was open for 1% -> 0% of each run, Pallas kernels for 0% -> 0%
where the time goes in v2:
time: 120 us; the launch traced here: 119 us
  Pallas kernels  116 us (97%)
  local copies, waits for them, and re-layouts  2.78 us (2%)
    pallas_call x1, Pallas kernels, on_device(): pl.pallas_call(screen_kernel, out_shape=jax.ShapeDtypeStruct((64, mrows),...  116 us
    unnamed x2, local copies, waits for them, and re-layouts  2.78 us

profile of v2, /device:TPU:1, one launch (start us, length us, event | category | flops | bytes accessed | tf_op | source)
XLA Modules:
  0.0 118.8 jit_solution(5878690387680738704)
XLA Ops:
  0.0 1.4 %copy.8.ratings = f32[128,4]{1,0:T(8,128)} copy(f32[128,4]{0,1:T(4,128)} %param.13) | data formatting | bytes 4096 | tf_op args[6]
  1.4 116.0 %screen.1 = f32[64,128]{1,0:T(8,128)} custom-call(f32[16,7552]{1,0:T(8,128)} %inj.1, f32[128,7552]{1,0:T(8,128)} %mon.1, f32[64,7552]{1,0:T(8,128)} %out.1, s32[1,2048]{1,0:T(1,128)} %bitcast.3, s32[1,2048]{1,0:T(1,128)} %bitcast.4, s32[1,64]{1,0:T(1,128)} %bitcast.5, f32[128,4]{1,0:T(8,128)} %copy.8.ratings), custom_call_target="tpu_custom_call" | custom-call | tf_op jit(solution)/shard_map/screen/pallas_call | solution.py:435
  117.4 1.4 %copy.10 = f32[64,128]{1,0:T(8,128)} copy(f32[64,128]{1,0:T(8,128)} %screen.1) | data formatting | bytes 65536

commit v3 on v2

--- a/solution.py
+++ b/solution.py
@@ -22,7 +22,7 @@
     inj, mon, out, ids_from, ids_to, hour_ids, ratings,
     result,
     a, b32, bl, bthi, btlo, onehot, ahi, alo,
-    part, parts3, tot, qsum, lod, send_flow, recv_flow, packs, fscr,
+    part, parts3, tot, qsum, lod, flow, send_flow, recv_flow, packs, fscr, lscr, accs,
     zs, zr, ys, yr, cs, cr, bsem, xs, xr, fs, fr, pzs, pzr, pys, pyr, pcs, pcr,
 ):
     me = lax.axis_index("branch")
@@ -120,41 +120,62 @@
     def send_c(delta, yy, e):
         item = len(c_items)
         other = 0 if yy is y else 1
-        c_items.append((delta, other, e))
+        c_items.append((delta % 8, other, e))
         dst = chunk(delta, yy, p, e)
         src = inj.at[pl.ds(8 * e, 8)] if (delta == 0 and other == 0) else dst
         send(src, dst, cs.at[item], cr.at[item], mate)
 
     got_c = set()
 
-    def recv_c(deltas):
-        for item, (delta, other, e) in enumerate(c_items):
-            if delta in deltas and item not in got_c:
+    def recv_c(pieces):
+        for delta, other, e in pieces:
+            item = c_items.index((delta % 8, other, e))
+            if item not in got_c:
                 got_c.add(item)
                 arrived(chunk(delta, oy if other else y, 1 - p, e), cr.at[item])
 
     tiles = width // 128
 
-    def block(deltas):
-        rows = 64 * len(deltas)
-        for n, delta in enumerate(deltas):
-            hi, lo = split_bf16(a[slot(delta)].reshape(64, width))
-            ahi[pl.ds(64 * n, 64)] = hi
-            alo[pl.ds(64 * n, 64)] = lo
-        top = pl.ds(0, rows)
+    def block(pieces):
+        recv_c(pieces)
+        for n, (delta, other, e) in enumerate(pieces):
+            hi, lo = split_bf16(a[slot(delta), oy if other else y, :, e].reshape(16, width))
+            ahi[pl.ds(16 * n, 16)] = hi
+            alo[pl.ds(16 * n, 16)] = lo
+        top = pl.ds(0, 16 * len(pieces))
         acc = jnp.dot(ahi[top], bthi[...], preferred_element_type=F32)
         acc = acc + jnp.dot(alo[top], bthi[...], preferred_element_type=F32)
         acc = acc + jnp.dot(ahi[top], btlo[...], preferred_element_type=F32)
-        for n, delta in enumerate(deltas):
+        for n, (delta, other, e) in enumerate(pieces):
+            for pp in range(2):
+                row = pl.multiple_of(32 * (oy if other else y) + 16 * pp + 8 * e, 8)
+                flow[slot(delta), pl.ds(row, 8)] = acc[16 * n + 8 * pp:16 * n + 8 * pp + 8]
+
+    def flow_copy(delta):
+        to = slot(delta)
+        k = (to - bus + 8) % 8
+        return k, pltpu.make_async_remote_copy(
+            src_ref=send_flow.at[to], dst_ref=recv_flow.at[k],
+            send_sem=fs.at[delta % 8], recv_sem=fr.at[k],
+            device_id={"bus": to}, device_id_type=MESH,
+        )
+
+    def finish(deltas):
+        for delta in deltas:
             k = slot(delta)
-            got = acc[64 * n:64 * n + 64]
-            send_flow[k, pl.ds(0, 64)] = got[:, :mrows]
-            tail = got[:, mrows:]
+            send_flow[k, pl.ds(0, 64)] = flow[k, :, pl.ds(0, mrows)]
+            tail = flow[k, :, pl.ds(mrows, orows)]
             send_flow[k, pl.ds(64, 32)] = jnp.concatenate([tail[:32], tail[32:]], axis=1)
+        for delta in deltas:
+            away, copy = flow_copy(delta)
+
+            @pl.when(away != 0)
+            def _():
+                copy.start()
 
     shift = bus * width
 
-    def transposed_b():
+    def transposed_b(first, last):
         def step(j, _):
             cols = pl.ds(pl.multiple_of(j * 128, 128), 128)
             for r, n in ((0, mrows), (mrows, orows)):
@@ -163,7 +184,7 @@
                 btlo[cols, pl.ds(r, n)] = lo
             return 0
 
-        lax.fori_loop(0, tiles, step, 0)
+        lax.fori_loop(first, last, step, 0)
 
     def left_b():
         for r in range(0, mrows, 32):
@@ -176,7 +197,9 @@
         f = ids_from[:, cols] - shift
         t = ids_to[:, cols] - shift
         same = f == t
-        return jnp.where(same, -1, f), jnp.where(same, -1, t)
+        f = jnp.where(same | (f < 0) | (f >= width), -1, f)
+        t = jnp.where(same | (t < 0) | (t >= width), -1, t)
+        return f, t
 
     def self_part():
         chip = me // 2
@@ -203,13 +226,16 @@
     def sens_part(d, half):
         i = (x + d) % 4
         f, t = index_rows(i * 512 + half * 256, 256)
-        sub = lax.broadcasted_iota(jnp.int32, (128, 256), 0)
+        f = jnp.broadcast_to(f, (128, 256)).astype(jnp.int16)
+        t = jnp.broadcast_to(t, (128, 256)).astype(jnp.int16)
+        sub = lax.broadcasted_iota(jnp.int32, (128, 256), 0).astype(jnp.int16)
+        one, zero = jnp.ones((128, 256), BF16), jnp.zeros((128, 256), BF16)
 
         def step(j, _):
-            at = sub + j * 128
+            at = sub + (j * 128).astype(jnp.int16)
             onehot[pl.ds(pl.multiple_of(j * 128, 128), 128)] = jnp.where(
-                f == at, 1.0, jnp.where(t == at, -1.0, 0.0)
-            ).astype(BF16)
+                f == at, one, jnp.where(t == at, -one, zero)
+            )
             return 0
 
         lax.fori_loop(0, tiles, step, 0)
@@ -266,158 +292,190 @@
     sens_part(2, 0)
     q = recv_both(0)
     both(send_z, 2)
-    q += [recv_y(0)]
-    run(q)
+    run(q + [recv_y(0)])
     sens_part(2, 1)
     send_part(2)
+    sens_part(1, 0)
     q = recv_both(1)
     both(send_z, 3)
     send_y(2), send_y(3)
-    q += [recv_y(1)]
-    both(send_z, 7)
-    run(q)
-    sens_part(1, 0)
+    run(q + [recv_y(1)])
     sens_part(1, 1)
     send_part(1)
+    sens_part(3, 0)
     q = recv_both(2)
     both(send_z, 4)
     run(q)
-    sens_part(3, 0)
     sens_part(3, 1)
     send_part(3)
     q = recv_both(3)
-    both(send_z, 5)
+    both(send_z, 5, 7)
     send_y(4), send_y(5)
-    q += [recv_y(2), recv_y(3)]
-    run(q)
+    run(q + [recv_y(2), recv_y(3)])
     sens_part(0, 0)
+    sens_part(0, 1)
+    q = [recv_z(0, 4)]
+    send_z(0, 6)
+    run(q + [recv_z(1, 4)])
+    sum_part()
+    pair_send.append(len(sends) - 1)
+    self_part()
+    transposed_b(0, tiles // 2)
+    q = recv_both(5)
+    send_z(1, 6)
+    send_y(6), send_y(7)
+    run(q + [recv_y(4), recv_y(5)])
+    transposed_b(tiles // 2, tiles)
+    share_part()
     q = recv_both(7)
     both(send_z, 8)
     run(q)
-    sens_part(0, 1)
-    sum_part()
-    pair_send.append(len(sends) - 1)
-    q = [recv_z(0, 4)]
-    send_z(0, 6)
-    q += [recv_z(1, 4)]
-    run(q)
-    self_part()
-    transposed_b()
-    share_part()
-    q = recv_both(5)
-    send_z(1, 6)
-    send_y(6), send_y(7)
-    q += [recv_y(4), recv_y(5)]
-    run(q)
+    block([(d, o, e) for d in (0, 1, -1) for o in (0, 1) for e in (0, 1)])
+    finish((0, 1, -1))
+    q = [recv_z(0, 6), recv_z(1, 6)]
+    send_y(8), send_y(9)
+    run(q + [recv_y(6), recv_y(7)])
+    block([(d, 0, e) for d in (3, -3, 4) for e in (0, 1)] + [(3, 1, 1), (-3, 1, 1)])
     q = recv_both(8)
     both(send_z, 9)
     run(q)
-    recv_c((0, 1, -1))
-    block((0,))
-    q = [recv_z(0, 6)]
-    send_y(8)
-    q += [recv_z(1, 6)]
-    send_y(9)
-    run(q)
-    block((1, -1))
-    run([recv_y(6), recv_y(7)])
-    recv_c((2, -2))
-    block((2, -2))
-    run(recv_both(9) + [recv_y(8), recv_y(9)])
-    recv_c((3, -3, 4, -4))
-    block((3, -3, -4))
-
-    for k in range(1, 8):
-        to = (bus + k) % 8
-        send(send_flow.at[to], recv_flow.at[k], fs.at[k], fr.at[k], {"bus": to})
-    own = send_flow[bus]
-    for k in range(1, 8):
-        arrived(recv_flow.at[k], fr.at[k])
-        own = own + recv_flow[k]
-    recv_flow[0] = own
-    packs[z, y, p] = recv_flow[0, pl.ds(64, 40)]
-
-    def pack_to_y(k, zz):
-        send(packs.at[zz, y, p], packs.at[zz, y, p], pys.at[k], pyr.at[k], across)
-
-    def pack_to_c(k, zz, yy):
-        send(packs.at[zz, yy, p], packs.at[zz, yy, p], pcs.at[k], pcr.at[k], mate)
-
-    for k in (4, 3, 5, 2, 6, 1, 7):
-        send(packs.at[z, y, p], packs.at[z, y, p], pzs.at[k], pzr.at[k], {"branch": (me + 4 * k) % 32})
-    pack_to_y(0, z)
-    pack_to_c(0, z, y)
-    order = (1, 7, 2, 6, 3, 5, 4)
-    for k in order:
-        zz = (z + 8 - k) % 8
-        arrived(packs.at[zz, y, p], pzr.at[k])
-        pack_to_y(k, zz)
-        pack_to_c(k, zz, y)
-    for k in (0,) + order:
-        zz = (z + 8 - k) % 8
-        arrived(packs.at[zz, oy, p], pyr.at[k])
-        pack_to_c(8 + k, zz, oy)
-    for k in (0,) + order:
-        zz = (z + 8 - k) % 8
-        arrived(packs.at[zz, y, 1 - p], pcr.at[k])
-        arrived(packs.at[zz, oy, 1 - p], pcr.at[8 + k])
-    take_part()
+    block([(d, o, e) for d in (2, -2) for o in (0, 1) for e in (0, 1)])
+    finish((2, -2))
+
+    def pack_z(k):
+        return pltpu.make_async_remote_copy(
+            src_ref=packs.at[z, y, p], dst_ref=packs.at[z, y, p], send_sem=pzs.at[k], recv_sem=pzr.at[k],
+            device_id={"branch": (me + 4 * k) % 32}, device_id_type=MESH,
+        )
+
+    def own_sum():
+        own = send_flow[bus]
+        for k in range(1, 8):
+            arrived(recv_flow.at[k], fr.at[k])
+            own = own + recv_flow[k]
+        recv_flow[0] = own
+        packs[z, y, p] = own[64:]
+        for k in (4, 3, 5, 2, 6, 1, 7):
+            pack_z(k).start()
+
+    order = (0, 1, 7, 2, 6, 3, 5, 4)
+
+    def forward_z():
+        for k in order:
+            zz = (z - k + 8) % 8
+            ref = packs.at[zz, y, p]
+            if k:
+                arrived(ref, pzr.at[k])
+            send(ref, ref, pys.at[k], pyr.at[k], across)
+            send(ref, ref, pcs.at[k], pcr.at[k], mate)
+
+    def forward_y():
+        for k in order:
+            ref = packs.at[(z - k + 8) % 8, oy, p]
+            arrived(ref, pyr.at[k])
+            send(ref, ref, pcs.at[8 + k], pcr.at[8 + k], mate)
 
     low = lax.broadcasted_iota(jnp.int32, (1, 128), 1) < 64
 
-    def unpack(n, _):
-        zz, yy = n // 2, n % 2
-        p0, p1 = packs[zz, yy, 0], packs[zz, yy, 1]
-        r0, r1 = pltpu.roll(p0, 64, 1), pltpu.roll(p1, 64, 1)
-        first = jnp.where(low, p0, r1)
-        second = jnp.where(low, r0, p1)
-        scale = 1.0 / jnp.maximum(1.0 - first[32:33], 0.25)
-        fscr[n, pl.ds(0, 32)] = first[:32] * scale
-        fscr[n, pl.ds(32, 32)] = second[:32] * scale
-        return 0
-
-    lax.fori_loop(0, 16, unpack, 0)
+    def take_lod():
+        for n, k in enumerate(order):
+            zz = (z - k + 8) % 8
+            for yy in range(2):
+                cols = pl.ds(pl.multiple_of((zz % 2 * 2 + yy) * 128, 128), 128)
+                lscr[2 * n + yy] = lod[zz // 2, :, cols]
+
+    def take_packs():
+        for n, k in enumerate(order):
+            zz = (z - k + 8) % 8
+            arrived(packs.at[zz, y, 1 - p], pcr.at[k])
+            arrived(packs.at[zz, oy, 1 - p], pcr.at[8 + k])
+            for yy in range(2):
+                at = 2 * n + yy
+                p0, p1 = packs[zz, yy, 0], packs[zz, yy, 1]
+                r0, r1 = pltpu.roll(p0, 64, 1), pltpu.roll(p1, 64, 1)
+                one = jnp.where(low, p0, r1)
+                two = jnp.where(low, r0, p1)
+                scale = 1.0 / jnp.maximum(1.0 - one[32:33], 0.25)
+                fscr[at, pl.ds(0, 32)] = one[:32] * scale
+                fscr[at, pl.ds(32, 32)] = two[:32] * scale
 
     lane = lax.broadcasted_iota(jnp.int32, (1, 1, 128), 2)
     hb, mt = 4, 4
 
-    def screen_m(g, _):
-        rows = pl.ds(pl.multiple_of(g * (8 * mt), 8 * mt), 8 * mt)
-
-        def screen_h(n, carry):
-            top, bot = carry
-            hi = [jnp.zeros((mt, 8, 128), F32) for _ in range(hb)]
-            lo = [jnp.zeros((mt, 8, 128), F32) for _ in range(hb)]
-            for kb in range(16):
-                l = lod[kb // 4, rows, pl.ds((kb % 4) * 128, 128)].reshape(mt, 8, 128)
+    def screen(first, last, g0, g1):
+        def screen_m(g, _):
+            rows = pl.ds(pl.multiple_of(g * (8 * mt), 8 * mt), 8 * mt)
+
+            def reduce_last(n, carry):
+                top, bot = carry
                 for i in range(hb):
-                    f = fscr[kb, pl.ds(n * hb + i, 8, stride=0)]
-                    v = l * f[None]
-                    hi[i] = jnp.maximum(hi[i], v)
-                    lo[i] = jnp.minimum(lo[i], v)
-            for i in range(hb):
-                here = lane == n * hb + i
-                top = jnp.where(here, jnp.max(hi[i], axis=2, keepdims=True), top)
-                bot = jnp.where(here, jnp.min(lo[i], axis=2, keepdims=True), bot)
-            return top, bot
-
-        zero = jnp.zeros((mt, 8, 128), F32)
-        top, bot = lax.fori_loop(0, 64 // hb, screen_h, (zero, zero))
-        parts3[0, rows, pl.ds(0, 128)] = top.reshape(8 * mt, 128)
-        parts3[1, rows, pl.ds(0, 128)] = bot.reshape(8 * mt, 128)
-        return 0
-
-    lax.fori_loop(0, mrows // (8 * mt), screen_m, 0)
-    base = jnp.concatenate([recv_flow[0, pl.ds(0, 64)], jnp.zeros((64, 128), F32)], axis=0).T
+                    here = lane == (n - 1) * hb + i
+                    most = jnp.max(accs[0, i], axis=2, keepdims=True)
+                    least = jnp.min(accs[1, i], axis=2, keepdims=True)
+                    top = jnp.maximum(top, jnp.where(here, most, 0.0))
+                    bot = jnp.minimum(bot, jnp.where(here, least, 0.0))
+                return top, bot
+
+            def screen_h(n, carry):
+                carry = reduce_last(n, carry)
+                hi = [jnp.zeros((mt, 8, 128), F32) for _ in range(hb)]
+                lo = [jnp.zeros((mt, 8, 128), F32) for _ in range(hb)]
+                for kb in range(first, last):
+                    l = lscr[kb, rows].reshape(mt, 8, 128)
+                    for i in range(hb):
+                        f = fscr[kb, pl.ds(n * hb + i, 8, stride=0)]
+                        v = l * f[None]
+                        hi[i] = jnp.maximum(hi[i], v)
+                        lo[i] = jnp.minimum(lo[i], v)
+                for i in range(hb):
+                    accs[0, i] = hi[i]
+                    accs[1, i] = lo[i]
+                return carry
+
+            zero = jnp.zeros((mt, 8, 128), F32)
+            accs[...] = jnp.zeros(accs.shape, F32)
+            carry = lax.fori_loop(0, 64 // hb, screen_h, (zero, zero))
+            top, bot = reduce_last(64 // hb, carry)
+            parts3[0, rows, pl.ds(0, 128)] = top.reshape(8 * mt, 128)
+            parts3[1, rows, pl.ds(0, 128)] = bot.reshape(8 * mt, 128)
+            return 0
+
+        lax.fori_loop(g0, g1, screen_m, 0)
+
+    groups = mrows // (8 * mt)
+
+    for item in (8, 9):
+        recv_y(item)()
+    for d in (0, 1):
+        recv_z(d, 9)()
+    block([(3, 1, 0), (-3, 1, 0), (4, 1, 0), (4, 1, 1)])
+    finish((3, -3, 4))
+    own_sum()
+    take_part()
+    take_lod()
+    forward_z()
+    forward_y()
+    take_packs()
+    screen(0, 16, 0, groups)
+    base = recv_flow[0, pl.ds(0, 64)]
     worst = jnp.maximum(
-        jnp.abs(base + parts3[0, :, pl.ds(0, 128)]), jnp.abs(base + parts3[1, :, pl.ds(0, 128)])
+        jnp.abs(base + parts3[0, :, pl.ds(0, 128)].T[:64]), jnp.abs(base + parts3[1, :, pl.ds(0, 128)].T[:64])
     )
     hour = jnp.concatenate([hour_ids[...], jnp.zeros((1, 64), jnp.int32)], axis=1)
-    season = (hour * 4) // 8760
-    rating = jnp.where(season == 0, ratings[:, 0:1], ratings[:, 1:2])
-    rating = jnp.where(season == 2, ratings[:, 2:3], rating)
-    rating = jnp.where(season == 3, ratings[:, 3:4], rating)
-    result[...] = (worst / rating).T[:64]
+    season = ((jnp.broadcast_to(hour, (128, 128)).T)[:64] * 4) // 8760
+    rating = jnp.where(season == 0, ratings[0:1], ratings[1:2])
+    rating = jnp.where(season == 2, ratings[2:3], rating)
+    rating = jnp.where(season == 3, ratings[3:4], rating)
+    result[...] = worst / rating
+    for k in range(1, 8):
+        pack_z(k).wait_send()
+    for delta in range(8):
+        away, copy = flow_copy(delta)
+
+        @pl.when(away != 0)
+        def _():
+            copy.wait_send()
+
     done = set(pair_send)
     for n, c in enumerate(sends):
         if n not in done:
@@ -451,10 +509,13 @@
             v((mrows, 512), F32),
             v((mrows, 512), F32),
             v((4, mrows, 512), F32),
+            v((8, 64, rows), F32),
             v((8, 104, 128), F32),
             v((8, 104, 128), F32),
             v((8, 2, 2, 40, 128), F32),
             v((16, 64, 128), F32),
+            v((16, mrows, 128), F32),
+            v((2, 4, 4, 8, 128), F32),
             dma((2, 10)), dma((2, 10)), dma((10,)), dma((10,)), dma((32,)), dma((32,)), dma((4,)),
             dma((7,)), dma((7,)), dma((8,)), dma((8,)), dma((8,)), dma((8,)), dma((8,)), dma((8,)),
             dma((16,)), dma((16,)),
@@ -465,7 +526,7 @@
         name="screen",
     )(
         injections, ptdf_mon, ptdf_out, outage_from.reshape(1, -1), outage_to.reshape(1, -1),
-        hour_ids.reshape(1, -1), ratings,
+        hour_ids.reshape(1, -1), ratings.T,
     )
 
 

time: 120 us -> 113 us (0.942)
  Pallas kernels: 116 us -> 111 us
  local copies, waits for them, and re-layouts: 2.78 us -> 1.38 us
    pallas_call x1, Pallas kernels: 116 us -> 111 us  [on_device(): pl.pallas_call(screen_kernel, out_shape=jax.ShapeDtypeStruct((64, mrows),...]
    unnamed x2 -> x1, local copies, waits for them, and re-layouts: 2.78 us -> 1.38 us
where the time goes in v3:
time: 113 us; the launch traced here: 112 us
  Pallas kernels  111 us (98%)
  local copies, waits for them, and re-layouts  1.38 us (1%)
    pallas_call x1, Pallas kernels, on_device(): pl.pallas_call(screen_kernel, out_shape=jax.ShapeDtypeStruct((64, mrows),...  111 us

profile of v3, /device:TPU:1, one launch (start us, length us, event | category | flops | bytes accessed | tf_op | source)
XLA Modules:
  0.0 112.4 jit_solution(2542453178394539320)
XLA Ops:
  0.0 111.0 %screen.1 = f32[64,128]{1,0:T(8,128)} custom-call(f32[16,7552]{1,0:T(8,128)} %inj.1, f32[128,7552]{1,0:T(8,128)} %mon.1, f32[64,7552]{1,0:T(8,128)} %out.1, s32[1,2048]{1,0:T(1,128)} %bitcast.4, s32[1,2048]{1,0:T(1,128)} %bitcast.5, s32[1,64]{1,0:T(1,128)} %bitcast.7, f32[4,128]{1,0:T(4,128)} %bitcast.6), custom_call_target="tpu_custom_call" | custom-call | tf_op jit(solution)/shard_map/screen/pallas_call | solution.py:493
  111.0 1.4 %copy.9 = f32[64,128]{1,0:T(8,128)} copy(f32[64,128]{1,0:T(8,128)} %screen.1) | data formatting | bytes 65536

commit v4 on v3

--- a/solution.py
+++ b/solution.py
@@ -339,8 +339,8 @@
     q = recv_both(8)
     both(send_z, 9)
     run(q)
-    block([(d, o, e) for d in (2, -2) for o in (0, 1) for e in (0, 1)])
-    finish((2, -2))
+    near, middle, far = (0, 1, -1), (2, -2), (3, -3, 4)
+    is_near = (bus - z + 9) % 8 < 3
 
     def pack_z(k):
         return pltpu.make_async_remote_copy(
@@ -358,39 +358,33 @@
         for k in (4, 3, 5, 2, 6, 1, 7):
             pack_z(k).start()
 
-    order = (0, 1, 7, 2, 6, 3, 5, 4)
-
-    def forward_z():
-        for k in order:
-            zz = (z - k + 8) % 8
-            ref = packs.at[zz, y, p]
-            if k:
-                arrived(ref, pzr.at[k])
-            send(ref, ref, pys.at[k], pyr.at[k], across)
-            send(ref, ref, pcs.at[k], pcr.at[k], mate)
-
-    def forward_y():
-        for k in order:
-            ref = packs.at[(z - k + 8) % 8, oy, p]
-            arrived(ref, pyr.at[k])
-            send(ref, ref, pcs.at[8 + k], pcr.at[8 + k], mate)
+    def forward_z(which):
+        for d in which:
+            zz = (bus + d + 8) % 8
+            k = (z - zz + 8) % 8
+
+            @pl.when(k != 0)
+            def _():
+                arrived(packs.at[zz, y, p], pzr.at[k])
+
+            send(packs.at[zz, y, p], packs.at[zz, y, p], pys.at[d % 8], pyr.at[d % 8], across)
+            send(packs.at[zz, y, p], packs.at[zz, y, p], pcs.at[d % 8], pcr.at[d % 8], mate)
+
+    def forward_y(which):
+        for d in which:
+            zz = (bus + d + 8) % 8
+            arrived(packs.at[zz, oy, p], pyr.at[d % 8])
+            send(packs.at[zz, oy, p], packs.at[zz, oy, p], pcs.at[8 + d % 8], pcr.at[8 + d % 8], mate)
 
     low = lax.broadcasted_iota(jnp.int32, (1, 128), 1) < 64
 
-    def take_lod():
-        for n, k in enumerate(order):
-            zz = (z - k + 8) % 8
+    def take_packs(which, first):
+        for n, d in enumerate(which):
+            zz = (bus + d + 8) % 8
+            arrived(packs.at[zz, y, 1 - p], pcr.at[d % 8])
+            arrived(packs.at[zz, oy, 1 - p], pcr.at[8 + d % 8])
             for yy in range(2):
-                cols = pl.ds(pl.multiple_of((zz % 2 * 2 + yy) * 128, 128), 128)
-                lscr[2 * n + yy] = lod[zz // 2, :, cols]
-
-    def take_packs():
-        for n, k in enumerate(order):
-            zz = (z - k + 8) % 8
-            arrived(packs.at[zz, y, 1 - p], pcr.at[k])
-            arrived(packs.at[zz, oy, 1 - p], pcr.at[8 + k])
-            for yy in range(2):
-                at = 2 * n + yy
+                at = first + 2 * n + yy
                 p0, p1 = packs[zz, yy, 0], packs[zz, yy, 1]
                 r0, r1 = pltpu.roll(p0, 64, 1), pltpu.roll(p1, 64, 1)
                 one = jnp.where(low, p0, r1)
@@ -398,6 +392,8 @@
                 scale = 1.0 / jnp.maximum(1.0 - one[32:33], 0.25)
                 fscr[at, pl.ds(0, 32)] = one[:32] * scale
                 fscr[at, pl.ds(32, 32)] = two[:32] * scale
+                cols = pl.ds(pl.multiple_of((zz % 2 * 2 + yy) * 128, 128), 128)
+                lscr[at] = lod[zz // 2, :, cols]
 
     lane = lax.broadcasted_iota(jnp.int32, (1, 1, 128), 2)
     hb, mt = 4, 4
@@ -432,9 +428,12 @@
                     accs[1, i] = lo[i]
                 return carry
 
-            zero = jnp.zeros((mt, 8, 128), F32)
+            if first == 0:
+                start = (jnp.zeros((mt, 8, 128), F32), jnp.zeros((mt, 8, 128), F32))
+            else:
+                start = tuple(parts3[i, rows, pl.ds(0, 128)].reshape(mt, 8, 128) for i in range(2))
             accs[...] = jnp.zeros(accs.shape, F32)
-            carry = lax.fori_loop(0, 64 // hb, screen_h, (zero, zero))
+            carry = lax.fori_loop(0, 64 // hb, screen_h, start)
             top, bot = reduce_last(64 // hb, carry)
             parts3[0, rows, pl.ds(0, 128)] = top.reshape(8 * mt, 128)
             parts3[1, rows, pl.ds(0, 128)] = bot.reshape(8 * mt, 128)
@@ -444,19 +443,35 @@
 
     groups = mrows // (8 * mt)
 
+    @pl.when(is_near)
+    def _():
+        own_sum()
+
+    block([(d, o, e) for d in (2, -2) for o in (0, 1) for e in (0, 1)])
+    finish((2, -2))
     for item in (8, 9):
         recv_y(item)()
     for d in (0, 1):
         recv_z(d, 9)()
     block([(3, 1, 0), (-3, 1, 0), (4, 1, 0), (4, 1, 1)])
     finish((3, -3, 4))
-    own_sum()
+    forward_z(near)
     take_part()
-    take_lod()
-    forward_z()
-    forward_y()
-    take_packs()
-    screen(0, 16, 0, groups)
+    forward_y(near)
+    take_packs(near, 0)
+
+    @pl.when(jnp.logical_not(is_near))
+    def _():
+        own_sum()
+
+    screen(0, 6, 0, groups)
+    forward_z(middle)
+    forward_z(far)
+    forward_y(middle)
+    forward_y(far)
+    take_packs(middle, 6)
+    take_packs(far, 10)
+    screen(6, 16, 0, groups)
     base = recv_flow[0, pl.ds(0, 64)]
     worst = jnp.maximum(
         jnp.abs(base + parts3[0, :, pl.ds(0, 128)].T[:64]), jnp.abs(base + parts3[1, :, pl.ds(0, 128)].T[:64])

time: 113 us -> 113 us (level)
  no operation moved by 1% of the time
where the time goes in v4:
time: 113 us
  Pallas kernels  111 us (98%)
  local copies, waits for them, and re-layouts  1.38 us (1%)
    pallas_call x1, Pallas kernels, on_device(): pl.pallas_call(screen_kernel, out_shape=jax.ShapeDtypeStruct((64, mrows),...  111 us

profile of v4, /device:TPU:1, one launch (start us, length us, event | category | flops | bytes accessed | tf_op | source)
XLA Modules:
  0.0 112.6 jit_solution(16320075365322734793)
XLA Ops:
  0.0 111.3 %screen.1 = f32[64,128]{1,0:T(8,128)} custom-call(f32[16,7552]{1,0:T(8,128)} %inj.1, f32[128,7552]{1,0:T(8,128)} %mon.1, f32[64,7552]{1,0:T(8,128)} %out.1, s32[1,2048]{1,0:T(1,128)} %bitcast.4, s32[1,2048]{1,0:T(1,128)} %bitcast.5, s32[1,64]{1,0:T(1,128)} %bitcast.7, f32[4,128]{1,0:T(4,128)} %bitcast.6), custom_call_target="tpu_custom_call" | custom-call | tf_op jit(solution)/shard_map/screen/pallas_call | solution.py:508
  111.3 1.4 %copy.9 = f32[64,128]{1,0:T(8,128)} copy(f32[64,128]{1,0:T(8,128)} %screen.1) | data formatting | bytes 65536
